TPU v7x, 32 devices: a whole 2x2x4 slice. The times are simulated.
32 devices in a mesh: grp: 2 (over x), pop: 16 (over z, y, core).
Axes of the slice: x: 2, y: 2, z: 4, core: 2. Of those that a mesh axis runs over, the one named last changes fastest.
Arguments:
- inputs: bfloat16 [64, 5120], P('grp'), parts along dimension 0, may hold values from -6 to 6
- gate_weight: bfloat16 [5120, 13824], P(None, 'pop'), may hold values from -0.078125 to 0.078125
- up_weight: bfloat16 [5120, 13824], P(None, 'pop'), may hold values from -0.078125 to 0.078125
- member_seeds: int32 [128], P(('grp', 'pop')), parts along dimension 0, may hold values from 0 to 1048575
- member_ranks: int32 [128], P(('grp', 'pop')), parts along dimension 0, may hold values from 0 to 63, each once
Outputs:
- hidden: bfloat16 [128, 32, 13824], P(('grp', 'pop')), parts along dimension 0
- gate_update: bfloat16 [10240, 13824], P('grp', 'pop'), parts along dimension 0
- up_update: bfloat16 [10240, 13824], P('grp', 'pop'), parts along dimension 0
There are 2 independent parts, one for each index of `grp`. A program takes and returns all parts, laid end to end along the dimension named above; an argument that names none is the same for every part. Nothing has to cross between parts.
Inputs may be any that keep to these rules, and one draw needn't show every extreme that they name: member_ranks holds each number from 0 to 63 once.
All inputs are finite; a program needn't handle non-finite values.
Results may differ from a plain program's by a relative error of at most 0.012.
Values may be sent and summed in bfloat16 or wider, within the bound.
No kernel may reach another device: no remote copies, remote signals or barrier semaphores. Data moves between devices by JAX's collectives and lax.ppermute only.
A program may use at most 128 MiB of HBM per device.

v0:
```python
import functools
import math

import jax
import jax.numpy as jnp
from jax import lax
from jax.experimental import pallas as pl
from jax.experimental.pallas import tpu as pltpu
from jax.sharding import PartitionSpec as P


R = 4
HASH_MULTIPLIER = 73244475
NOISE_SCALE = math.sqrt(3.0) / 32768.0
PERTURB = 0.3
MINOR = (((1,), (1,)), ((), ()))


def high(value):
    return lax.shift_right_logical(value, jnp.int32(16))


def scramble(value):
    value = (value ^ high(value)) * HASH_MULTIPLIER
    value = (value ^ high(value)) * HASH_MULTIPLIER
    return value ^ high(value)


def mixed(value):
    value = scramble(value)
    return value ^ high(value)


def centered(mix):
    value = mix * HASH_MULTIPLIER
    value = (value ^ high(value)) * HASH_MULTIPLIER
    return ((value ^ high(value)) & 65535).astype(jnp.float32) - 32767.5


def entries(start, rows, length):
    row = lax.broadcasted_iota(jnp.int32, (rows, length), 0)
    column = lax.broadcasted_iota(jnp.int32, (rows, length), 1) + start
    return mixed(column * R + (row & (R - 1)) + 1)


def own_keys(seeds_ref, stream, first):
    row = lax.broadcasted_iota(jnp.int32, (8, 128), 0)
    low = mixed(seeds_ref[first] * 4 + stream)
    top = mixed(seeds_ref[first + 1] * 4 + stream)
    return jnp.where(row < R, low, top)


def own_noise(seeds_ref, stream, hashes, length):
    pieces = []
    for first in range(0, seeds_ref.shape[0], 2):
        key = own_keys(seeds_ref, stream, first)
        pieces.append(
            jnp.concatenate(
                [centered(hashes[:, q : q + 128] ^ key) for q in range(0, length, 128)], axis=1
            )
        )
    return jnp.concatenate(pieces, axis=0).astype(jnp.bfloat16)


SCALARS = pl.BlockSpec(memory_space=pltpu.SMEM)
WHOLE = pl.BlockSpec(memory_space=pltpu.VMEM)
PLACED = pl.BlockSpec(memory_space=pl.ANY)


def room(mebibytes):
    return pltpu.CompilerParams(vmem_limit_bytes=mebibytes * 2**20)


def base_kernel(
    seeds_ref, ranks_ref, x_ref, gate_ref, up_ref, out_ref, info_ref, own, x_buf, gate_buf, up_buf, small, sems, *, pieces, ahead
):
    seq = x_buf.shape[0]
    first = [
        pltpu.make_async_copy(x_ref, x_buf, small.at[0]),
        pltpu.make_async_copy(seeds_ref, own.at[0], small.at[1]),
        pltpu.make_async_copy(ranks_ref, own.at[1], small.at[2]),
    ]
    copies = []
    begin = 0
    for i, size in enumerate(pieces):
        part = pl.ds(begin, size)
        copies.append(
            (
                pltpu.make_async_copy(gate_ref.at[:, part], gate_buf.at[:, part], sems.at[0, i]),
                pltpu.make_async_copy(up_ref.at[:, part], up_buf.at[:, part], sems.at[1, i]),
            )
        )
        begin += size
    for copy in first:
        copy.start()
    for pair in copies[:ahead]:
        for copy in pair:
            copy.start()
    for copy in first:
        copy.wait()
    local = own.shape[1]
    row = lax.broadcasted_iota(jnp.int32, info_ref.shape, 0)
    lane = lax.broadcasted_iota(jnp.int32, info_ref.shape, 1) - lax.axis_index("pop") * local
    info = jnp.zeros(info_ref.shape, jnp.int32)
    for m in range(local):
        value = jnp.where(row == 0, own[0, m], jnp.where(row == 1, own[1, m], 0))
        info = jnp.where(lane == m, value, info)
    info_ref[...] = info
    sums = [None, None]
    begin = 0
    for i, size in enumerate(pieces):
        for copy in copies[i]:
            copy.wait()
        if i + ahead < len(pieces):
            for copy in copies[i + ahead]:
                copy.start()
        part = slice(begin, begin + size)
        for s, buf in enumerate((gate_buf, up_buf)):
            term = lax.dot_general(
                x_buf[:, part], buf[:, part], MINOR, preferred_element_type=jnp.float32
            )
            sums[s] = term if sums[s] is None else sums[s] + term
        begin += size
    for s in range(2):
        out_ref[s * seq : (s + 1) * seq] = sums[s].astype(jnp.bfloat16)


def base_projections(seeds, ranks, inputs, gate_rows, up_rows, lanes):
    seq, depth = inputs.shape
    width = gate_rows.shape[0]
    pieces = (512,) + (1024,) * (depth // 1024 - 1) + (512,)
    return pl.pallas_call(
        functools.partial(base_kernel, pieces=pieces, ahead=3),
        out_shape=(
            jax.ShapeDtypeStruct((2 * seq, width), jnp.bfloat16),
            jax.ShapeDtypeStruct((8, lanes), jnp.int32),
        ),
        in_specs=[PLACED] * 5,
        out_specs=(WHOLE, WHOLE),
        scratch_shapes=[
            pltpu.SMEM((2, seeds.shape[0]), jnp.int32),
            pltpu.VMEM((seq, depth), jnp.bfloat16),
            pltpu.VMEM((width, depth), jnp.bfloat16),
            pltpu.VMEM((width, depth), jnp.bfloat16),
            pltpu.SemaphoreType.DMA((3,)),
            pltpu.SemaphoreType.DMA((2, len(pieces))),
        ],
        compiler_params=room(57),
        cost_estimate=pl.CostEstimate(
            flops=4 * seq * depth * width, bytes_accessed=4 * depth * width, transcendentals=0
        ),
        name="base",
    )(seeds, ranks, inputs, gate_rows, up_rows)


def coeff_kernel(seeds_ref, x_ref, out_ref):
    seq, depth = x_ref.shape
    members = seeds_ref.shape[0]
    rows = members * R
    scale = NOISE_SCALE / math.sqrt(depth) * (PERTURB / math.sqrt(R)) * NOISE_SCALE
    hashes = entries(0, 8, depth)
    x = x_ref[...]
    row = lax.broadcasted_iota(jnp.int32, (members * seq, rows + seq), 0)
    lane = lax.broadcasted_iota(jnp.int32, (members * seq, rows + seq), 1)
    own = (row // seq) == (lane // R)
    pick = (lane - rows) == (row % seq)
    for s in range(2):
        noise = own_noise(seeds_ref, 2 * s, hashes, depth)
        padded = jnp.concatenate([noise, jnp.zeros((seq, depth), jnp.bfloat16)], axis=0)
        coeff = lax.dot_general(x, padded, MINOR, preferred_element_type=jnp.float32) * scale
        tiled = jnp.concatenate([coeff] * members, axis=0)
        out_ref[s] = jnp.where(
            lane < rows, jnp.where(own, tiled, 0.0), jnp.where(pick, 1.0, 0.0)
        ).astype(jnp.bfloat16)


def left_operands(seeds, inputs):
    seq = inputs.shape[0]
    members = seeds.shape[0]
    return pl.pallas_call(
        coeff_kernel,
        out_shape=jax.ShapeDtypeStruct((2, members * seq, members * R + seq), jnp.bfloat16),
        in_specs=[SCALARS, WHOLE],
        out_specs=WHOLE,
        compiler_params=room(12),
        cost_estimate=pl.CostEstimate(flops=10**7, bytes_accessed=10**6, transcendentals=0),
        name="coeff",
    )(seeds, inputs)


def noise_kernel(seeds_ref, out_ref, *, part):
    for start in range(0, out_ref.shape[2], part):
        hashes = entries(start, 8, part)
        for s in range(2):
            out_ref[s, :, start : start + part] = own_noise(seeds_ref, 2 * s + 1, hashes, part)


def output_noise(seeds, total):
    return pl.pallas_call(
        functools.partial(noise_kernel, part=1536),
        out_shape=jax.ShapeDtypeStruct((2, seeds.shape[0] * R, total), jnp.bfloat16),
        in_specs=[SCALARS],
        out_specs=WHOLE,
        compiler_params=room(8),
        cost_estimate=pl.CostEstimate(flops=10**7, bytes_accessed=10**6, transcendentals=0),
        name="noise",
    )(seeds)


def chip_at(place, chips):
    if chips <= 8:
        return jnp.where(place < chips // 2, 2 * place, 2 * (chips - 1 - place) + 1)
    return place


def ring_place(chip, chips):
    if chips <= 8:
        return jnp.where(chip % 2 == 0, chip // 2, chips - 1 - chip // 2)
    return chip


def hidden_kernel(left_ref, noise_ref, *rest, seq, sub, chunk):
    shard_refs, (out_ref, ordered, base, buf, sems) = rest[:-5], rest[-5:]
    chips = len(shard_refs)
    reach = chips // 2
    width = base.shape[1] // (2 * chips)
    group = 128 // math.gcd(width, 128)
    position = lax.axis_index("pop")
    core = lax.rem(position, 2)
    here = ring_place(position // 2, chips)
    for i, ref in enumerate(shard_refs):
        step = i if i <= reach else i - reach
        toward = 2 * core - 1 if i <= reach else 1 - 2 * core
        chip = chip_at(lax.rem(here + toward * step + chips, chips), chips)
        owner = core if i <= reach else 1 - core
        for c in range(2):
            ordered[2 * chip + (owner if c == 0 else 1 - owner)] = ref[c]
    for first in range(0, 2 * chips, group):
        base[:, first * width : (first + group) * width] = jnp.concatenate(
            [ordered[shard] for shard in range(first, first + group)], axis=1
        )
    copies = []
    for begin in range(0, out_ref.shape[1], sub):
        part = slice(begin, begin + sub)
        totals = []
        for s in range(2):
            right = jnp.concatenate(
                [noise_ref[s, :, part], base[s * seq : (s + 1) * seq, part]], axis=0
            )
            totals.append(jnp.dot(left_ref[s], right, preferred_element_type=jnp.float32))
        half = 0.5 * totals[0]
        buf[:, part] = ((half + half * jnp.tanh(half)) * totals[1]).astype(jnp.bfloat16)
        if (begin + sub) % chunk == 0:
            i = begin // chunk
            span = pl.ds(i * chunk, chunk)
            copies.append(
                pltpu.make_async_copy(buf.at[:, span], out_ref.at[:, span], sems.at[i])
            )
            copies[-1].start()
    for copy in copies:
        copy.wait()


def hidden_states(left, noise, shards, width, seq, sub=256, chunk=1536):
    rows = left.shape[1]
    total = noise.shape[2]
    return pl.pallas_call(
        functools.partial(hidden_kernel, seq=seq, sub=sub, chunk=chunk),
        out_shape=jax.ShapeDtypeStruct((rows, total), jnp.bfloat16),
        in_specs=[WHOLE] * (2 + len(shards)),
        out_specs=PLACED,
        scratch_shapes=[
            pltpu.VMEM((2 * len(shards), 2 * seq, width), jnp.bfloat16),
            pltpu.VMEM((2 * seq, total), jnp.bfloat16),
            pltpu.VMEM((rows, total), jnp.bfloat16),
            pltpu.SemaphoreType.DMA((total // chunk,)),
        ],
        compiler_params=room(16),
        cost_estimate=pl.CostEstimate(
            flops=10**8, bytes_accessed=6 * 10**6, transcendentals=2 * 10**6
        ),
        name="hidden",
    )(left, noise, *shards)


def columns_kernel(info_ref, got_ref, cols_ref, keys_ref, *, population):
    width, terms = cols_ref.shape[1:]
    norm = NOISE_SCALE * NOISE_SCALE / math.sqrt(population * R)
    info = info_ref[...] + got_ref[...]
    seeds = info[0:1, 0:population]
    ranks = info[1:2, 0:population]
    scale = ((ranks.astype(jnp.float32) + 0.5) / population - 0.5) * norm
    scales = jnp.concatenate([scale] * R, axis=1)
    wide = jnp.concatenate([seeds] * R, axis=1)
    for s in range(2):
        for t in range(0, population, 64):
            square = jnp.broadcast_to(seeds[:, t : t + 64].astype(jnp.float32), (128, 64))
            keys_ref[s, t : t + 64, :] = mixed(square.T.astype(jnp.int32) * 4 + 2 * s)
    lane_keys = [mixed(wide * 4 + (2 * s + 1)) for s in range(2)]
    part = width // 9
    offset = lax.axis_index("pop") * width

    def fill(r, carry):
        column = lax.broadcasted_iota(jnp.int32, (part, 128), 0) + (offset + r * part)
        lane = lax.broadcasted_iota(jnp.int32, (part, 128), 1)
        where = pl.ds(pl.multiple_of(r * part, 8), part)
        for t in range(0, terms, 128):
            hashes = mixed(column * R + (lane + t) // population + 1)
            for s in range(2):
                noise = centered(hashes ^ lane_keys[s][:, t : t + 128])
                cols_ref[s, where, t : t + 128] = (noise * scales[:, t : t + 128]).astype(jnp.bfloat16)
        return carry

    lax.fori_loop(0, 9, fill, 0)


def update_columns(info, got, population, width):
    return pl.pallas_call(
        functools.partial(columns_kernel, population=population),
        out_shape=(
            jax.ShapeDtypeStruct((2, width, population * R), jnp.bfloat16),
            jax.ShapeDtypeStruct((2, population, 128), jnp.int32),
        ),
        in_specs=[WHOLE, WHOLE],
        out_specs=(WHOLE, WHOLE),
        compiler_params=room(8),
        cost_estimate=pl.CostEstimate(flops=10**7, bytes_accessed=10**6, transcendentals=0),
        name="columns",
    )(info, got)


def update_kernel(keys_ref, cols_ref, out_ref, buf, rows_buf, sems, *, stream, sub, chunk):
    depth = out_ref.shape[1]
    population = keys_ref.shape[1]

    def generate(j):
        hashes = entries(j * sub, 8, sub)
        slot = j % 2
        for k in range(R):
            for q in range(0, sub, 128):
                entry = jnp.broadcast_to(hashes[k : k + 1, q : q + 128], (16, 128))
                for t in range(0, population, 16):
                    at = k * population + t
                    rows_buf[slot, at : at + 16, q : q + 128] = centered(
                        entry ^ keys_ref[stream, t : t + 16, :]
                    ).astype(jnp.bfloat16)

    count = depth // sub
    copies = []
    generate(0)
    for j in range(count):
        if j + 1 < count:
            generate(j + 1)
        buf[:, j * sub : (j + 1) * sub] = jnp.dot(
            cols_ref[stream], rows_buf[j % 2], preferred_element_type=jnp.float32
        ).astype(jnp.bfloat16)
        if (j + 1) * sub % chunk == 0:
            i = j * sub // chunk
            span = pl.ds(i * chunk, chunk)
            copies.append(
                pltpu.make_async_copy(buf.at[:, span], out_ref.at[:, span], sems.at[i])
            )
            copies[-1].start()
    for copy in copies:
        copy.wait()


def update(keys, cols, stream, depth, sub=256, chunk=512):
    width, terms = cols.shape[1:]
    return pl.pallas_call(
        functools.partial(update_kernel, stream=stream, sub=sub, chunk=chunk),
        out_shape=jax.ShapeDtypeStruct((width, depth), jnp.bfloat16),
        in_specs=[WHOLE, WHOLE],
        out_specs=PLACED,
        scratch_shapes=[
            pltpu.VMEM((width, depth), jnp.bfloat16),
            pltpu.VMEM((2, terms, sub), jnp.bfloat16),
            pltpu.SemaphoreType.DMA((depth // chunk,)),
        ],
        compiler_params=room(24),
        cost_estimate=pl.CostEstimate(
            flops=2 * width * terms * depth, bytes_accessed=2 * width * depth, transcendentals=0
        ),
        name="update",
    )(keys, cols)


def ring_order(chips):
    if chips <= 8:
        return list(range(0, chips, 2)) + list(range(chips - 1, 0, -2))
    return list(range(chips))


def together(*values):
    return lax.optimization_barrier(values)


def per_device(inputs, gate_weight, up_weight, member_seeds, member_ranks):
    devices = lax.axis_size("pop")
    depth, width = gate_weight.shape
    local = member_seeds.shape[0]
    seq = inputs.shape[0]
    population = devices * local
    chips = devices // 2
    order = ring_order(chips)
    siblings = [(i, i ^ 1) for i in range(devices)]
    onward = [
        (2 * order[i] + c, 2 * order[(i + 1 - 2 * c) % chips] + c) for i in range(chips) for c in range(2)
    ]

    base, info = base_projections(
        member_seeds, member_ranks, inputs, gate_weight.T, up_weight.T, -(-population // 128) * 128
    )

    def named(value, pairs):
        return lax.ppermute(value, "pop", pairs)

    def seed_step(info, stride):
        return named(info, [(i, i ^ stride) for i in range(devices)])

    got = seed_step(info, 1)
    sibling = lax.ppermute(base, "pop", siblings)
    left = left_operands(member_seeds, together(inputs, base)[0])
    info, base, sibling, left = together(info + got, base, sibling, left)
    stride = 2
    got = seed_step(info, stride)
    moving = jnp.stack([base, sibling])
    arrived, crossed = [moving], []
    noise = output_noise(together(member_seeds, moving)[0], devices * width)
    cols = keys = None
    updates = [None, None]
    for k in range(1, chips // 2 + 1):
        onto = named(moving, onward)
        if k == 1:
            onto, noise = together(onto, noise)
        else:
            crossed.append(lax.ppermute(moving, "pop", siblings))
        if cols is None and 2 * stride < devices:
            info = info + got
            stride *= 2
            got = seed_step(info, stride)
        elif cols is None:
            cols, keys = update_columns(*together(info, got, moving)[:2], population, width)
            updates[0] = update(keys, cols, 0, depth)
            onto, cols, first = together(onto, cols, updates[0])
            updates[0] = first
        elif updates[1] is None:
            updates[1] = update(keys, cols, 1, depth)
        moving = onto
        arrived.append(moving)
    noise = together(noise, *updates)[0]
    hidden = hidden_states(left, noise, arrived + crossed, width, seq)
    return (hidden.reshape(local, seq, -1), updates[0].T, updates[1].T)


def solution(mesh):
    placed = (P("grp", None), P(None, "pop"), P(None, "pop"), P(("grp", "pop")), P(("grp", "pop")))
    return jax.shard_map(
        per_device,
        mesh=mesh,
        in_specs=placed,
        out_specs=(P(("grp", "pop"), None, None), P("grp", "pop"), P("grp", "pop")),
        check_vma=False,
    )
```

profile of v0, /device:TPU:0, one launch (start us, length us, event | category | flops | bytes accessed | tf_op | source)
XLA Modules:
  0.0 49.6 jit_solution(17847299794682159732)
XLA Ops:
  0.6 0.0 copy-start
  0.6 0.0 copy-start.1
  0.7 8.9 %base.1 = (bf16[64,864]{1,0:T(8,128)(2,1)}, s32[8,128]{1,0:T(8,128)}) custom-call(s32[4]{0:T(128)} %seeds_ref.4, s32[4]{0:T(128)} %ranks_ref.1, bf16[32,5120]{1,0:T(8,128)(2,1)} %x_ref.2, bf16[864,5120]{1,0:T(8,128)(2,1)} %bitcast.9, bf16[864,5120]{1,0:T(8,128)(2,1)} %bitcast.10), custom_call_target="tpu_custom_call" | custom-call | flops 566231040 | bytes 17694720 | tf_op jit(solution)/shard_map/base/pallas_call | solution.py:132
  9.6 0.6 %collective-permute-start.1 = (bf16[64,864]{1,0:T(8,128)(2,1)}, bf16[64,864]{1,0:T(8,128)(2,1)S(1)}, u32[]{:S(2)}, u32[]{:S(2)}) collective-permute-start(bf16[64,864]{1,0:T(8,128)(2,1)} %get-tuple-element.25), channel_id=1, source_target_pairs={{0,1},{1,0},{2,3},{3,2},{4,5},{5,4},{6,7},{7,6},{8,9},{9,8},{10,11... | collective-permute-start | bytes 331784 | tf_op jit(solution)/shard_map/ppermute | solution.py:422
  10.1 0.1 collective-permute-start
  10.2 0.0 copy-done
  10.2 0.0 copy-done.1
  10.2 1.0 %coeff.1.left_ref = bf16[2,128,48]{2,1,0:T(8,128)(2,1)S(1)} custom-call(s32[4]{0:T(128)S(1)} %copy-done.1, bf16[32,5120]{1,0:T(8,128)(2,1)S(1)} %copy-done), custom_call_target="tpu_custom_call" | custom-call | flops 10000000 | bytes 1000000 | tf_op jit(solution)/shard_map/coeff/pallas_call | solution.py:180
  11.3 0.3 collective-permute-done
  11.5 0.7 %add.9 = s32[8,128]{1,0:T(8,128)S(1)} add(s32[8,128]{1,0:T(8,128)} %get-tuple-element.21, s32[8,128]{1,0:T(8,128)S(1)} %collective-permute-done) | non-fusion elementwise | flops 1024 | bytes 12288 | tf_op jit(solution)/shard_map/add | solution.py:424
  12.2 0.0 collective-permute-done.1
  12.2 0.9 %pad_maximum_fusion.rest_0_ = bf16[2,64,864]{2,1,0:T(8,128)(2,1)S(1)} fusion(bf16[1,64,864]{2,1,0:T(8,128)(2,1)S(1)} %bitcast.13, bf16[1,64,864]{2,1,0:T(8,128)(2,1)} %bitcast.12), kind=kLoop, calls=%fused_computation | loop fusion | flops 110592 | bytes 442368 | tf_op jit(solution)/shard_map/stack | solution.py:427
  13.2 2.8 %collective-permute-start.2 = (bf16[2,64,864]{2,1,0:T(8,128)(2,1)S(1)}, bf16[2,64,864]{2,1,0:T(8,128)(2,1)S(1)}, u32[]{:S(2)}, u32[]{:S(2)}) collective-permute-start(bf16[2,64,864]{2,1,0:T(8,128)(2,1)S(1)} %pad_maximum_fusion.rest_0_), channel_id=1, source_target_pairs={{0,4},{1,3},{4,8},{5,1},{8,12},{9,5},{12,14},{13,9},{14,10},{15,13... | collective-permute-start | bytes 663560 | tf_op jit(solution)/shard_map/ppermute | solution.py:416
  15.9 1.4 %noise.1.noise_ref = bf16[2,16,13824]{2,1,0:T(8,128)(2,1)S(1)} custom-call(s32[4]{0:T(128)S(1)} %copy-done.1), custom_call_target="tpu_custom_call" | custom-call | flops 10000000 | bytes 1000000 | tf_op jit(solution)/shard_map/noise/pallas_call | solution.py:199
  17.3 2.6 %collective-permute-done.2.rest_1_ = bf16[2,64,864]{2,1,0:T(8,128)(2,1)S(1)} collective-permute-done((bf16[2,64,864]{2,1,0:T(8,128)(2,1)S(1)}, bf16[2,64,864]{2,1,0:T(8,128)(2,1)S(1)}, u32[]{:S(2)}, u32[]{:S(2)}) %collective-permute-start.2) | collective-permute-done | bytes 221216 | tf_op jit(solution)/shard_map/ppermute | solution.py:416
  19.9 2.1 %collective-permute-start.3 = (bf16[2,64,864]{2,1,0:T(8,128)(2,1)S(1)}, bf16[2,64,864]{2,1,0:T(8,128)(2,1)S(1)}, u32[]{:S(2)}, u32[]{:S(2)}) collective-permute-start(bf16[2,64,864]{2,1,0:T(8,128)(2,1)S(1)} %collective-permute-done.2.rest_1_), channel_id=1, source_target_pairs={{0,4},{1,3},{4,8},{5,1},{8,12},{9,5},{12,14},{13,9},{14,10},{15,13... | collective-permute-start | bytes 663560 | tf_op jit(solution)/shard_map/ppermute | solution.py:416
  22.0 0.0 collective-permute-start.5
  22.0 4.0 %collective-permute-done.5 = s32[8,128]{1,0:T(8,128)S(1)} collective-permute-done((s32[8,128]{1,0:T(8,128)S(1)}, s32[8,128]{1,0:T(8,128)S(1)}, u32[]{:S(2)}, u32[]{:S(2)}) %collective-permute-start.5) | collective-permute-done | bytes 4128 | tf_op jit(solution)/shard_map/ppermute | solution.py:416
  26.0 1.2 %collective-permute-start.6 = (s32[8,128]{1,0:T(8,128)S(1)}, s32[8,128]{1,0:T(8,128)S(1)}, u32[]{:S(2)}, u32[]{:S(2)}) collective-permute-start(s32[8,128]{1,0:T(8,128)S(1)} %add.10), channel_id=1, source_target_pairs={{0,4},{1,5},{2,6},{3,7},{4,0},{5,1},{6,2},{7,3},{8,12},{9,13},{10,... | collective-permute-start | bytes 12296 | tf_op jit(solution)/shard_map/ppermute | solution.py:416
  27.2 0.0 collective-permute-done.3.rest_2_
  27.2 0.9 %collective-permute-start.4 = (bf16[2,64,864]{2,1,0:T(8,128)(2,1)S(1)}, bf16[2,64,864]{2,1,0:T(8,128)(2,1)S(1)}, u32[]{:S(2)}, u32[]{:S(2)}) collective-permute-start(bf16[2,64,864]{2,1,0:T(8,128)(2,1)S(1)} %collective-permute-done.3.rest_2_), channel_id=1, source_target_pairs={{0,4},{1,3},{4,8},{5,1},{8,12},{9,5},{12,14},{13,9},{14,10},{15,13... | collective-permute-start | bytes 663560 | tf_op jit(solution)/shard_map/ppermute | solution.py:416
  28.0 1.6 %collective-permute-done.6 = s32[8,128]{1,0:T(8,128)S(1)} collective-permute-done((s32[8,128]{1,0:T(8,128)S(1)}, s32[8,128]{1,0:T(8,128)S(1)}, u32[]{:S(2)}, u32[]{:S(2)}) %collective-permute-start.6) | collective-permute-done | bytes 4128 | tf_op jit(solution)/shard_map/ppermute | solution.py:416
  29.7 2.2 %collective-permute-start.7 = (s32[8,128]{1,0:T(8,128)S(1)}, s32[8,128]{1,0:T(8,128)S(1)}, u32[]{:S(2)}, u32[]{:S(2)}) collective-permute-start(s32[8,128]{1,0:T(8,128)S(1)} %add.11.info_ref), channel_id=1, source_target_pairs={{0,8},{1,9},{2,10},{3,11},{4,12},{5,13},{6,14},{7,15},{8,0},{9,1},... | collective-permute-start | bytes 12296 | tf_op jit(solution)/shard_map/ppermute | solution.py:416
  31.8 0.0 collective-permute-start.9
  31.8 2.3 %collective-permute-done.7.got_ref = s32[8,128]{1,0:T(8,128)S(1)} collective-permute-done((s32[8,128]{1,0:T(8,128)S(1)}, s32[8,128]{1,0:T(8,128)S(1)}, u32[]{:S(2)}, u32[]{:S(2)}) %collective-permute-start.7) | collective-permute-done | bytes 4128 | tf_op jit(solution)/shard_map/ppermute | solution.py:416
  34.2 0.0 collective-permute-start.10
  34.2 1.2 %columns.1 = (bf16[2,864,256]{2,1,0:T(8,128)(2,1)S(1)}, s32[2,64,128]{2,1,0:T(8,128)S(1)}) custom-call(s32[8,128]{1,0:T(8,128)S(1)} %add.11.info_ref, s32[8,128]{1,0:T(8,128)S(1)} %collective-permute-done.7.got_ref), custom_call_target="tpu_custom_call" | custom-call | flops 10000000 | bytes 1000000 | tf_op jit(solution)/shard_map/columns/pallas_call | solution.py:318
  35.4 4.5 %update.2 = bf16[864,5120]{1,0:T(8,128)(2,1)} custom-call(s32[2,64,128]{2,1,0:T(8,128)S(1)} %get-tuple-element.34.keys_ref, bf16[2,864,256]{2,1,0:T(8,128)(2,1)S(1)} %get-tuple-element.36.cols_ref), custom_call_target="tpu_custom_call" | custom-call | flops 2264924160 | bytes 8847360 | tf_op jit(solution)/shard_map/update/pallas_call | solution.py:370
  39.9 0.0 collective-permute-done.4.rest_3_
  39.9 0.6 %collective-permute-start.11 = (bf16[2,64,864]{2,1,0:T(8,128)(2,1)S(1)}, bf16[2,64,864]{2,1,0:T(8,128)(2,1)S(1)}, u32[]{:S(2)}, u32[]{:S(2)}) collective-permute-start(bf16[2,64,864]{2,1,0:T(8,128)(2,1)S(1)} %collective-permute-done.4.rest_3_), channel_id=1, source_target_pairs={{0,1},{1,0},{2,3},{3,2},{4,5},{5,4},{6,7},{7,6},{8,9},{9,8},{10,11... | collective-permute-start | bytes 663560 | tf_op jit(solution)/shard_map/ppermute | solution.py:437
  40.5 1.1 %collective-permute-start.8 = (bf16[2,64,864]{2,1,0:T(8,128)(2,1)S(1)}, bf16[2,64,864]{2,1,0:T(8,128)(2,1)S(1)}, u32[]{:S(2)}, u32[]{:S(2)}) collective-permute-start(bf16[2,64,864]{2,1,0:T(8,128)(2,1)S(1)} %collective-permute-done.4.rest_3_), channel_id=1, source_target_pairs={{0,4},{1,3},{4,8},{5,1},{8,12},{9,5},{12,14},{13,9},{14,10},{15,13... | collective-permute-start | bytes 663560 | tf_op jit(solution)/shard_map/ppermute | solution.py:416
  41.6 4.5 %update.3 = bf16[864,5120]{1,0:T(8,128)(2,1)} custom-call(s32[2,64,128]{2,1,0:T(8,128)S(1)} %get-tuple-element.34.keys_ref, bf16[2,864,256]{2,1,0:T(8,128)(2,1)S(1)} %get-tuple-element.36.cols_ref), custom_call_target="tpu_custom_call" | custom-call | flops 2264924160 | bytes 8847360 | tf_op jit(solution)/shard_map/update/pallas_call | solution.py:370
  46.1 0.0 collective-permute-done.9.rest_5_
  46.1 0.0 collective-permute-done.10.rest_6_
  46.1 0.0 collective-permute-done.11.rest_7_
  46.1 0.4 collective-permute-done.8.rest_4_
  46.5 3.0 %hidden.1 = bf16[128,13824]{1,0:T(8,128)(2,1)} custom-call(bf16[2,128,48]{2,1,0:T(8,128)(2,1)S(1)} %coeff.1.left_ref, bf16[2,16,13824]{2,1,0:T(8,128)(2,1)S(1)} %noise.1.noise_ref, bf16[2,64,864]{2,1,0:T(8,128)(2,1)S(1)} %pad_maximum_fusion.rest_0_, bf16[2,64,864]{2,1,0:T(8,128)(2,1)S(1)} %collective-permute-done.2.rest_1_, ...), custom_call_target="tpu_custom_call" | custom-call | flops 100000000 | bytes 6000000 | tf_op jit(solution)/shard_map/hidden/pallas_call | solution.py:267
  (2 shorter events, 0.0 us)
Async XLA Ops:
  0.6 9.6 %copy-start = (bf16[32,5120]{1,0:T(8,128)(2,1)S(1)}, bf16[32,5120]{1,0:T(8,128)(2,1)}, u32[]{:S(2)}) copy-start(bf16[32,5120]{1,0:T(8,128)(2,1)} %x_ref.2) | copy-start | bytes 983044
  0.6 9.6 %copy-start.1 = (s32[4]{0:T(128)S(1)}, s32[4]{0:T(128)}, u32[]{:S(2)}) copy-start(s32[4]{0:T(128)} %seeds_ref.4) | copy-start | bytes 52
  9.6 2.6 %collective-permute-start.1 = (bf16[64,864]{1,0:T(8,128)(2,1)}, bf16[64,864]{1,0:T(8,128)(2,1)S(1)}, u32[]{:S(2)}, u32[]{:S(2)}) collective-permute-start(bf16[64,864]{1,0:T(8,128)(2,1)} %get-tuple-element.25), channel_id=1, source_target_pairs={{0,1},{1,0},{2,3},{3,2},{4,5},{5,4},{6,7},{7,6},{8,9},{9,8},{10,11... | collective-permute-start | bytes 331784 | tf_op jit(solution)/shard_map/ppermute | solution.py:422
  10.1 1.4 %collective-permute-start = (s32[8,128]{1,0:T(8,128)}, s32[8,128]{1,0:T(8,128)S(1)}, u32[]{:S(2)}, u32[]{:S(2)}) collective-permute-start(s32[8,128]{1,0:T(8,128)} %get-tuple-element.21), channel_id=1, source_target_pairs={{0,1},{1,0},{2,3},{3,2},{4,5},{5,4},{6,7},{7,6},{8,9},{9,8},{10,11... | collective-permute-start | bytes 12296 | tf_op jit(solution)/shard_map/ppermute | solution.py:416
  13.2 6.7 %collective-permute-start.2 = (bf16[2,64,864]{2,1,0:T(8,128)(2,1)S(1)}, bf16[2,64,864]{2,1,0:T(8,128)(2,1)S(1)}, u32[]{:S(2)}, u32[]{:S(2)}) collective-permute-start(bf16[2,64,864]{2,1,0:T(8,128)(2,1)S(1)} %pad_maximum_fusion.rest_0_), channel_id=1, source_target_pairs={{0,4},{1,3},{4,8},{5,1},{8,12},{9,5},{12,14},{13,9},{14,10},{15,13... | collective-permute-start | bytes 663560 | tf_op jit(solution)/shard_map/ppermute | solution.py:416
  19.9 7.3 %collective-permute-start.3 = (bf16[2,64,864]{2,1,0:T(8,128)(2,1)S(1)}, bf16[2,64,864]{2,1,0:T(8,128)(2,1)S(1)}, u32[]{:S(2)}, u32[]{:S(2)}) collective-permute-start(bf16[2,64,864]{2,1,0:T(8,128)(2,1)S(1)} %collective-permute-done.2.rest_1_), channel_id=1, source_target_pairs={{0,4},{1,3},{4,8},{5,1},{8,12},{9,5},{12,14},{13,9},{14,10},{15,13... | collective-permute-start | bytes 663560 | tf_op jit(solution)/shard_map/ppermute | solution.py:416
  22.0 4.0 %collective-permute-start.5 = (s32[8,128]{1,0:T(8,128)S(1)}, s32[8,128]{1,0:T(8,128)S(1)}, u32[]{:S(2)}, u32[]{:S(2)}) collective-permute-start(s32[8,128]{1,0:T(8,128)S(1)} %add.9), channel_id=1, source_target_pairs={{0,2},{1,3},{2,0},{3,1},{4,6},{5,7},{6,4},{7,5},{8,10},{9,11},{10,... | collective-permute-start | bytes 12296 | tf_op jit(solution)/shard_map/ppermute | solution.py:416
  26.0 3.7 %collective-permute-start.6 = (s32[8,128]{1,0:T(8,128)S(1)}, s32[8,128]{1,0:T(8,128)S(1)}, u32[]{:S(2)}, u32[]{:S(2)}) collective-permute-start(s32[8,128]{1,0:T(8,128)S(1)} %add.10), channel_id=1, source_target_pairs={{0,4},{1,5},{2,6},{3,7},{4,0},{5,1},{6,2},{7,3},{8,12},{9,13},{10,... | collective-permute-start | bytes 12296 | tf_op jit(solution)/shard_map/ppermute | solution.py:416
  27.2 12.7 %collective-permute-start.4 = (bf16[2,64,864]{2,1,0:T(8,128)(2,1)S(1)}, bf16[2,64,864]{2,1,0:T(8,128)(2,1)S(1)}, u32[]{:S(2)}, u32[]{:S(2)}) collective-permute-start(bf16[2,64,864]{2,1,0:T(8,128)(2,1)S(1)} %collective-permute-done.3.rest_2_), channel_id=1, source_target_pairs={{0,4},{1,3},{4,8},{5,1},{8,12},{9,5},{12,14},{13,9},{14,10},{15,13... | collective-permute-start | bytes 663560 | tf_op jit(solution)/shard_map/ppermute | solution.py:416
  29.7 4.5 %collective-permute-start.7 = (s32[8,128]{1,0:T(8,128)S(1)}, s32[8,128]{1,0:T(8,128)S(1)}, u32[]{:S(2)}, u32[]{:S(2)}) collective-permute-start(s32[8,128]{1,0:T(8,128)S(1)} %add.11.info_ref), channel_id=1, source_target_pairs={{0,8},{1,9},{2,10},{3,11},{4,12},{5,13},{6,14},{7,15},{8,0},{9,1},... | collective-permute-start | bytes 12296 | tf_op jit(solution)/shard_map/ppermute | solution.py:416
  31.8 14.2 %collective-permute-start.9 = (bf16[2,64,864]{2,1,0:T(8,128)(2,1)S(1)}, bf16[2,64,864]{2,1,0:T(8,128)(2,1)S(1)}, u32[]{:S(2)}, u32[]{:S(2)}) collective-permute-start(bf16[2,64,864]{2,1,0:T(8,128)(2,1)S(1)} %collective-permute-done.2.rest_1_), channel_id=1, source_target_pairs={{0,1},{1,0},{2,3},{3,2},{4,5},{5,4},{6,7},{7,6},{8,9},{9,8},{10,11... | collective-permute-start | bytes 663560 | tf_op jit(solution)/shard_map/ppermute | solution.py:437
  34.2 11.9 %collective-permute-start.10 = (bf16[2,64,864]{2,1,0:T(8,128)(2,1)S(1)}, bf16[2,64,864]{2,1,0:T(8,128)(2,1)S(1)}, u32[]{:S(2)}, u32[]{:S(2)}) collective-permute-start(bf16[2,64,864]{2,1,0:T(8,128)(2,1)S(1)} %collective-permute-done.3.rest_2_), channel_id=1, source_target_pairs={{0,1},{1,0},{2,3},{3,2},{4,5},{5,4},{6,7},{7,6},{8,9},{9,8},{10,11... | collective-permute-start | bytes 663560 | tf_op jit(solution)/shard_map/ppermute | solution.py:437
  39.9 6.2 %collective-permute-start.11 = (bf16[2,64,864]{2,1,0:T(8,128)(2,1)S(1)}, bf16[2,64,864]{2,1,0:T(8,128)(2,1)S(1)}, u32[]{:S(2)}, u32[]{:S(2)}) collective-permute-start(bf16[2,64,864]{2,1,0:T(8,128)(2,1)S(1)} %collective-permute-done.4.rest_3_), channel_id=1, source_target_pairs={{0,1},{1,0},{2,3},{3,2},{4,5},{5,4},{6,7},{7,6},{8,9},{9,8},{10,11... | collective-permute-start | bytes 663560 | tf_op jit(solution)/shard_map/ppermute | solution.py:437
  40.5 6.0 %collective-permute-start.8 = (bf16[2,64,864]{2,1,0:T(8,128)(2,1)S(1)}, bf16[2,64,864]{2,1,0:T(8,128)(2,1)S(1)}, u32[]{:S(2)}, u32[]{:S(2)}) collective-permute-start(bf16[2,64,864]{2,1,0:T(8,128)(2,1)S(1)} %collective-permute-done.4.rest_3_), channel_id=1, source_target_pairs={{0,4},{1,3},{4,8},{5,1},{8,12},{9,5},{12,14},{13,9},{14,10},{15,13... | collective-permute-start | bytes 663560 | tf_op jit(solution)/shard_map/ppermute | solution.py:416
where the time goes:
time: 49.8 us; the launch traced here: 49.6 us
  Pallas kernels  24.5 us (49%)
  starting transfers between devices  11.4 us (23%)
  waiting for transfers between devices  11.2 us (22%)
  other arithmetic  1.63 us (3%)
  between operations  0.9 us (2%)
    ppermute x8, waiting for transfers between devices, named(): return lax.ppermute(value, 'pop', pairs)  11.2 us
    ppermute x8, starting transfers between devices, named(): return lax.ppermute(value, 'pop', pairs)  10.3 us
    pallas_call x1, Pallas kernels, base_projections(): pl.pallas_call(functools.partial(base_kernel, pieces=pieces, ahead=3), ou...  8.93 us
    pallas_call x2, Pallas kernels, update(): pl.pallas_call(functools.partial(update_kernel, stream=stream, sub=sub, c...  8.93 us
    pallas_call x1, Pallas kernels, hidden_states(): pl.pallas_call(functools.partial(hidden_kernel, seq=seq, sub=sub, chunk=c...  2.98 us
    pallas_call x1, Pallas kernels, output_noise(): pl.pallas_call(functools.partial(noise_kernel, part=1536), out_shape=jax....  1.36 us
    pallas_call x1, Pallas kernels, update_columns(): pl.pallas_call(functools.partial(columns_kernel, population=population),...  1.25 us
    pallas_call x1, Pallas kernels, left_operands(): pl.pallas_call(coeff_kernel, out_shape=jax.ShapeDtypeStruct((2, members *...  1.02 us
  transfers between devices with their start and end apart: 12, of which 6 were waited for; matrix products, arithmetic and copies ran while one was open for 1% of the time, Pallas kernels for 25%

commit v1 on v0

--- a/solution.py
+++ b/solution.py
@@ -153,10 +153,13 @@
     )(seeds, ranks, inputs, gate_rows, up_rows)
 
 
-def coeff_kernel(seeds_ref, x_ref, out_ref):
+def coeff_kernel(seeds_ref, x_ref, base_ref, info_ref, out_ref, pair_ref, kept_ref):
     seq, depth = x_ref.shape
     members = seeds_ref.shape[0]
     rows = members * R
+    pair_ref[0] = base_ref[...]
+    pair_ref[1] = base_ref[...]
+    kept_ref[...] = info_ref[...]
     scale = NOISE_SCALE / math.sqrt(depth) * (PERTURB / math.sqrt(R)) * NOISE_SCALE
     hashes = entries(0, 8, depth)
     x = x_ref[...]
@@ -174,33 +177,54 @@
         ).astype(jnp.bfloat16)
 
 
-def left_operands(seeds, inputs):
+def left_operands(seeds, inputs, base, info):
     seq = inputs.shape[0]
     members = seeds.shape[0]
     return pl.pallas_call(
         coeff_kernel,
-        out_shape=jax.ShapeDtypeStruct((2, members * seq, members * R + seq), jnp.bfloat16),
-        in_specs=[SCALARS, WHOLE],
-        out_specs=WHOLE,
+        out_shape=(
+            jax.ShapeDtypeStruct((2, members * seq, members * R + seq), jnp.bfloat16),
+            jax.ShapeDtypeStruct((2,) + base.shape, base.dtype),
+            jax.ShapeDtypeStruct(info.shape, info.dtype),
+        ),
+        in_specs=[SCALARS, WHOLE, WHOLE, WHOLE],
+        out_specs=(WHOLE, WHOLE, WHOLE),
         compiler_params=room(12),
         cost_estimate=pl.CostEstimate(flops=10**7, bytes_accessed=10**6, transcendentals=0),
         name="coeff",
-    )(seeds, inputs)
-
-
-def noise_kernel(seeds_ref, out_ref, *, part):
+    )(seeds, inputs, base, info)
+
+
+def noise_kernel(seeds_ref, out_ref, hash_ref, *, part, population):
+    tiles, width = hash_ref.shape[:2]
+    rows = width // 9
+    offset = lax.axis_index("pop") * width
+
+    def fill(r, carry):
+        column = lax.broadcasted_iota(jnp.int32, (rows, 128), 0) + (offset + r * rows)
+        lane = lax.broadcasted_iota(jnp.int32, (rows, 128), 1)
+        for t in range(tiles):
+            hash_ref[t, pl.ds(pl.multiple_of(r * rows, 8), rows), :] = mixed(
+                column * R + (lane + 128 * t) // population + 1
+            )
+        return carry
+
+    lax.fori_loop(0, 9, fill, 0)
     for start in range(0, out_ref.shape[2], part):
         hashes = entries(start, 8, part)
         for s in range(2):
             out_ref[s, :, start : start + part] = own_noise(seeds_ref, 2 * s + 1, hashes, part)
 
 
-def output_noise(seeds, total):
-    return pl.pallas_call(
-        functools.partial(noise_kernel, part=1536),
-        out_shape=jax.ShapeDtypeStruct((2, seeds.shape[0] * R, total), jnp.bfloat16),
+def output_noise(seeds, total, width, population):
+    return pl.pallas_call(
+        functools.partial(noise_kernel, part=1536, population=population),
+        out_shape=(
+            jax.ShapeDtypeStruct((2, seeds.shape[0] * R, total), jnp.bfloat16),
+            jax.ShapeDtypeStruct((population * R // 128, width, 128), jnp.int32),
+        ),
         in_specs=[SCALARS],
-        out_specs=WHOLE,
+        out_specs=(WHOLE, WHOLE),
         compiler_params=room(8),
         cost_estimate=pl.CostEstimate(flops=10**7, bytes_accessed=10**6, transcendentals=0),
         name="noise",
@@ -283,7 +307,7 @@
     )(left, noise, *shards)
 
 
-def columns_kernel(info_ref, got_ref, cols_ref, keys_ref, *, population):
+def columns_kernel(info_ref, got_ref, hash_ref, cols_ref, keys_ref, *, population):
     width, terms = cols_ref.shape[1:]
     norm = NOISE_SCALE * NOISE_SCALE / math.sqrt(population * R)
     info = info_ref[...] + got_ref[...]
@@ -298,14 +322,11 @@
             keys_ref[s, t : t + 64, :] = mixed(square.T.astype(jnp.int32) * 4 + 2 * s)
     lane_keys = [mixed(wide * 4 + (2 * s + 1)) for s in range(2)]
     part = width // 9
-    offset = lax.axis_index("pop") * width
 
     def fill(r, carry):
-        column = lax.broadcasted_iota(jnp.int32, (part, 128), 0) + (offset + r * part)
-        lane = lax.broadcasted_iota(jnp.int32, (part, 128), 1)
         where = pl.ds(pl.multiple_of(r * part, 8), part)
         for t in range(0, terms, 128):
-            hashes = mixed(column * R + (lane + t) // population + 1)
+            hashes = hash_ref[t // 128, where, :]
             for s in range(2):
                 noise = centered(hashes ^ lane_keys[s][:, t : t + 128])
                 cols_ref[s, where, t : t + 128] = (noise * scales[:, t : t + 128]).astype(jnp.bfloat16)
@@ -314,19 +335,19 @@
     lax.fori_loop(0, 9, fill, 0)
 
 
-def update_columns(info, got, population, width):
+def update_columns(info, got, hashes, population, width):
     return pl.pallas_call(
         functools.partial(columns_kernel, population=population),
         out_shape=(
             jax.ShapeDtypeStruct((2, width, population * R), jnp.bfloat16),
             jax.ShapeDtypeStruct((2, population, 128), jnp.int32),
         ),
-        in_specs=[WHOLE, WHOLE],
+        in_specs=[WHOLE, WHOLE, WHOLE],
         out_specs=(WHOLE, WHOLE),
         compiler_params=room(8),
         cost_estimate=pl.CostEstimate(flops=10**7, bytes_accessed=10**6, transcendentals=0),
         name="columns",
-    )(info, got)
+    )(info, got, hashes)
 
 
 def update_kernel(keys_ref, cols_ref, out_ref, buf, rows_buf, sems, *, stream, sub, chunk):
@@ -420,13 +441,15 @@
 
     got = seed_step(info, 1)
     sibling = lax.ppermute(base, "pop", siblings)
-    left = left_operands(member_seeds, together(inputs, base)[0])
-    info, base, sibling, left = together(info + got, base, sibling, left)
+    left, pair, info = left_operands(member_seeds, inputs, base, info)
+    info, pair, sibling, left = together(info + got, pair, sibling, left)
     stride = 2
     got = seed_step(info, stride)
-    moving = jnp.stack([base, sibling])
+    moving = lax.dynamic_update_slice(pair, sibling[None], (1, 0, 0))
     arrived, crossed = [moving], []
-    noise = output_noise(together(member_seeds, moving)[0], devices * width)
+    noise, hashes = output_noise(
+        together(member_seeds, moving)[0], devices * width, width, population
+    )
     cols = keys = None
     updates = [None, None]
     for k in range(1, chips // 2 + 1):
@@ -440,7 +463,9 @@
             stride *= 2
             got = seed_step(info, stride)
         elif cols is None:
-            cols, keys = update_columns(*together(info, got, moving)[:2], population, width)
+            cols, keys = update_columns(
+                *together(info, got, moving)[:2], hashes, population, width
+            )
             updates[0] = update(keys, cols, 0, depth)
             onto, cols, first = together(onto, cols, updates[0])
             updates[0] = first

time: 49.8 us -> 49.4 us (level)
  other arithmetic: 1.63 us -> 0.01 us
  local copies, waits for them, and re-layouts: 0.01 us -> 1.61 us
  waiting for transfers between devices: 11.2 us -> 10.5 us
    unnamed x4 -> x8, local copies, waits for them, and re-layouts: 0.01 us -> 1.59 us
    another operation x1 -> x0, other arithmetic: 0.93 us -> none  [per_device(): moving = jnp.stack([base, sibling])]
    ppermute x8, waiting for transfers between devices: 11.2 us -> 10.5 us  [named(): return lax.ppermute(value, 'pop', pairs)]
    add x1, other arithmetic: 0.69 us -> 0.01 us  [per_device(): info, pair, sibling, left = together(info + got, pair, sibling, left)]
  transfers between devices with their start and end apart: 12 -> 12, of which waited for: 6 -> 5; matrix products, arithmetic and copies ran while one was open for 1% -> 0% of each run, Pallas kernels for 25% -> 26%
where the time goes in v1:
time: 49.4 us; the launch traced here: 49.3 us
  Pallas kernels  24.5 us (50%)
  starting transfers between devices  11.7 us (24%)
  waiting for transfers between devices  10.5 us (21%)
  local copies, waits for them, and re-layouts  1.61 us (3%)
  between operations  0.93 us (2%)
    ppermute x8, starting transfers between devices, named(): return lax.ppermute(value, 'pop', pairs)  10.5 us
    ppermute x8, waiting for transfers between devices, named(): return lax.ppermute(value, 'pop', pairs)  10.5 us
    pallas_call x1, Pallas kernels, base_projections(): pl.pallas_call(functools.partial(base_kernel, pieces=pieces, ahead=3), ou...  8.93 us
    pallas_call x2, Pallas kernels, update(): pl.pallas_call(functools.partial(update_kernel, stream=stream, sub=sub, c...  8.93 us
    pallas_call x1, Pallas kernels, hidden_states(): pl.pallas_call(functools.partial(hidden_kernel, seq=seq, sub=sub, chunk=c...  2.98 us
    pallas_call x1, Pallas kernels, output_noise(): pl.pallas_call(functools.partial(noise_kernel, part=1536, population=popu...  1.81 us
    unnamed x8, local copies, waits for them, and re-layouts  1.59 us
    pallas_call x1, Pallas kernels, left_operands(): pl.pallas_call(coeff_kernel, out_shape=(jax.ShapeDtypeStruct((2, members...  1.05 us
  transfers between devices with their start and end apart: 12, of which 5 were waited for; matrix products, arithmetic and copies ran while one was open for 0% of the time, Pallas kernels for 26%

profile of v1, /device:TPU:0, one launch (start us, length us, event | category | flops | bytes accessed | tf_op | source)
XLA Modules:
  0.0 49.3 jit_solution(18003113634337988319)
XLA Ops:
  0.6 0.0 copy-start
  0.6 0.0 copy-start.3
  0.7 8.9 %base.1 = (bf16[64,864]{1,0:T(8,128)(2,1)}, s32[8,128]{1,0:T(8,128)}) custom-call(s32[4]{0:T(128)} %seeds_ref.4, s32[4]{0:T(128)} %ranks_ref.1, bf16[32,5120]{1,0:T(8,128)(2,1)} %x_ref.3, bf16[864,5120]{1,0:T(8,128)(2,1)} %bitcast.9, bf16[864,5120]{1,0:T(8,128)(2,1)} %bitcast.10), custom_call_target="tpu_custom_call" | custom-call | flops 566231040 | bytes 17694720 | tf_op jit(solution)/shard_map/base/pallas_call | solution.py:132
  9.6 0.6 %collective-permute-start.1 = (bf16[64,864]{1,0:T(8,128)(2,1)}, bf16[64,864]{1,0:T(8,128)(2,1)S(1)}, u32[]{:S(2)}, u32[]{:S(2)}) collective-permute-start(bf16[64,864]{1,0:T(8,128)(2,1)} %get-tuple-element.25.base_ref), channel_id=1, source_target_pairs={{0,1},{1,0},{2,3},{3,2},{4,5},{5,4},{6,7},{7,6},{8,9},{9,8},{10,11... | collective-permute-start | bytes 331784 | tf_op jit(solution)/shard_map/ppermute | solution.py:443
  10.1 0.1 collective-permute-start
  10.2 0.0 copy-done
  10.2 0.0 copy-done.3
  10.2 0.0 copy-start.1
  10.2 0.9 %copy-done.1 = bf16[64,864]{1,0:T(8,128)(2,1)S(1)} copy-done((bf16[64,864]{1,0:T(8,128)(2,1)S(1)}, bf16[64,864]{1,0:T(8,128)(2,1)}, u32[]{:S(2)}) %copy-start.1) | copy-done | bytes 110616
  11.1 0.0 copy-start.2
  11.1 0.7 %copy-done.2 = s32[8,128]{1,0:T(8,128)S(1)} copy-done((s32[8,128]{1,0:T(8,128)S(1)}, s32[8,128]{1,0:T(8,128)}, u32[]{:S(2)}) %copy-start.2) | copy-done | bytes 4120
  11.8 1.0 %coeff.1 = (bf16[2,128,48]{2,1,0:T(8,128)(2,1)S(1)}, bf16[2,64,864]{2,1,0:T(8,128)(2,1)S(1)}, s32[8,128]{1,0:T(8,128)S(1)}) custom-call(s32[4]{0:T(128)S(1)} %copy-done.3, bf16[32,5120]{1,0:T(8,128)(2,1)S(1)} %copy-done, bf16[64,864]{1,0:T(8,128)(2,1)S(1)} %copy-done.1, s32[8,128]{1,0:T(8,128)S(1)} %copy-done.2), custom_call_target="tpu_custom_call" | custom-call | flops 10000000 | bytes 1000000 | tf_op jit(solution)/shard_map/coeff/pallas_call | solution.py:183
  12.9 0.0 collective-permute-done
  12.9 0.0 collective-permute-done.1
  12.9 3.0 %collective-permute-start.2 = (bf16[2,64,864]{2,1,0:T(8,128)(2,1)S(1)}, bf16[2,64,864]{2,1,0:T(8,128)(2,1)S(1)}, u32[]{:S(2)}, u32[]{:S(2)}) collective-permute-start(bf16[2,64,864]{2,1,0:T(8,128)(2,1)S(1)} %bitcast_dynamic-update-slice_fusion.rest_0_), channel_id=1, source_target_pairs={{0,4},{1,3},{4,8},{5,1},{8,12},{9,5},{12,14},{13,9},{14,10},{15,13... | collective-permute-start | bytes 663560 | tf_op jit(solution)/shard_map/ppermute | solution.py:437
  16.0 1.8 %noise.1 = (bf16[2,16,13824]{2,1,0:T(8,128)(2,1)S(1)}, s32[2,864,128]{2,1,0:T(8,128)S(1)}) custom-call(s32[4]{0:T(128)S(1)} %copy-done.3), custom_call_target="tpu_custom_call" | custom-call | flops 10000000 | bytes 1000000 | tf_op jit(solution)/shard_map/noise/pallas_call | solution.py:220
  17.8 2.1 %collective-permute-done.2.rest_1_ = bf16[2,64,864]{2,1,0:T(8,128)(2,1)S(1)} collective-permute-done((bf16[2,64,864]{2,1,0:T(8,128)(2,1)S(1)}, bf16[2,64,864]{2,1,0:T(8,128)(2,1)S(1)}, u32[]{:S(2)}, u32[]{:S(2)}) %collective-permute-start.2) | collective-permute-done | bytes 221216 | tf_op jit(solution)/shard_map/ppermute | solution.py:437
  19.9 2.1 %collective-permute-start.3 = (bf16[2,64,864]{2,1,0:T(8,128)(2,1)S(1)}, bf16[2,64,864]{2,1,0:T(8,128)(2,1)S(1)}, u32[]{:S(2)}, u32[]{:S(2)}) collective-permute-start(bf16[2,64,864]{2,1,0:T(8,128)(2,1)S(1)} %collective-permute-done.2.rest_1_), channel_id=1, source_target_pairs={{0,4},{1,3},{4,8},{5,1},{8,12},{9,5},{12,14},{13,9},{14,10},{15,13... | collective-permute-start | bytes 663560 | tf_op jit(solution)/shard_map/ppermute | solution.py:437
  22.0 0.0 collective-permute-start.5
  22.0 4.0 %collective-permute-done.5 = s32[8,128]{1,0:T(8,128)S(1)} collective-permute-done((s32[8,128]{1,0:T(8,128)S(1)}, s32[8,128]{1,0:T(8,128)S(1)}, u32[]{:S(2)}, u32[]{:S(2)}) %collective-permute-start.5) | collective-permute-done | bytes 4128 | tf_op jit(solution)/shard_map/ppermute | solution.py:437
  26.0 1.2 %collective-permute-start.6 = (s32[8,128]{1,0:T(8,128)S(1)}, s32[8,128]{1,0:T(8,128)S(1)}, u32[]{:S(2)}, u32[]{:S(2)}) collective-permute-start(s32[8,128]{1,0:T(8,128)S(1)} %add.10), channel_id=1, source_target_pairs={{0,4},{1,5},{2,6},{3,7},{4,0},{5,1},{6,2},{7,3},{8,12},{9,13},{10,... | collective-permute-start | bytes 12296 | tf_op jit(solution)/shard_map/ppermute | solution.py:437
  27.2 0.0 collective-permute-done.3.rest_2_
  27.2 0.9 %collective-permute-start.4 = (bf16[2,64,864]{2,1,0:T(8,128)(2,1)S(1)}, bf16[2,64,864]{2,1,0:T(8,128)(2,1)S(1)}, u32[]{:S(2)}, u32[]{:S(2)}) collective-permute-start(bf16[2,64,864]{2,1,0:T(8,128)(2,1)S(1)} %collective-permute-done.3.rest_2_), channel_id=1, source_target_pairs={{0,4},{1,3},{4,8},{5,1},{8,12},{9,5},{12,14},{13,9},{14,10},{15,13... | collective-permute-start | bytes 663560 | tf_op jit(solution)/shard_map/ppermute | solution.py:437
  28.1 1.6 %collective-permute-done.6 = s32[8,128]{1,0:T(8,128)S(1)} collective-permute-done((s32[8,128]{1,0:T(8,128)S(1)}, s32[8,128]{1,0:T(8,128)S(1)}, u32[]{:S(2)}, u32[]{:S(2)}) %collective-permute-start.6) | collective-permute-done | bytes 4128 | tf_op jit(solution)/shard_map/ppermute | solution.py:437
  29.7 2.2 %collective-permute-start.7 = (s32[8,128]{1,0:T(8,128)S(1)}, s32[8,128]{1,0:T(8,128)S(1)}, u32[]{:S(2)}, u32[]{:S(2)}) collective-permute-start(s32[8,128]{1,0:T(8,128)S(1)} %add.11.info_ref), channel_id=1, source_target_pairs={{0,8},{1,9},{2,10},{3,11},{4,12},{5,13},{6,14},{7,15},{8,0},{9,1},... | collective-permute-start | bytes 12296 | tf_op jit(solution)/shard_map/ppermute | solution.py:437
  31.8 0.0 collective-permute-start.9
  31.8 2.3 %collective-permute-done.7.got_ref = s32[8,128]{1,0:T(8,128)S(1)} collective-permute-done((s32[8,128]{1,0:T(8,128)S(1)}, s32[8,128]{1,0:T(8,128)S(1)}, u32[]{:S(2)}, u32[]{:S(2)}) %collective-permute-start.7) | collective-permute-done | bytes 4128 | tf_op jit(solution)/shard_map/ppermute | solution.py:437
  34.2 0.0 collective-permute-start.10
  34.2 0.9 %columns.1 = (bf16[2,864,256]{2,1,0:T(8,128)(2,1)S(1)}, s32[2,64,128]{2,1,0:T(8,128)S(1)}) custom-call(s32[8,128]{1,0:T(8,128)S(1)} %add.11.info_ref, s32[8,128]{1,0:T(8,128)S(1)} %collective-permute-done.7.got_ref, s32[2,864,128]{2,1,0:T(8,128)S(1)} %get-tuple-element.40.hash_ref), custom_call_target="tpu_custom_call" | custom-call | flops 10000000 | bytes 1000000 | tf_op jit(solution)/shard_map/columns/pallas_call | solution.py:339
  35.0 4.5 %update.2 = bf16[864,5120]{1,0:T(8,128)(2,1)} custom-call(s32[2,64,128]{2,1,0:T(8,128)S(1)} %get-tuple-element.42.keys_ref, bf16[2,864,256]{2,1,0:T(8,128)(2,1)S(1)} %get-tuple-element.44.cols_ref), custom_call_target="tpu_custom_call" | custom-call | flops 2264924160 | bytes 8847360 | tf_op jit(solution)/shard_map/update/pallas_call | solution.py:391
  39.5 0.0 collective-permute-done.4.rest_3_
  39.5 0.6 %collective-permute-start.11 = (bf16[2,64,864]{2,1,0:T(8,128)(2,1)S(1)}, bf16[2,64,864]{2,1,0:T(8,128)(2,1)S(1)}, u32[]{:S(2)}, u32[]{:S(2)}) collective-permute-start(bf16[2,64,864]{2,1,0:T(8,128)(2,1)S(1)} %collective-permute-done.4.rest_3_), channel_id=1, source_target_pairs={{0,1},{1,0},{2,3},{3,2},{4,5},{5,4},{6,7},{7,6},{8,9},{9,8},{10,11... | collective-permute-start | bytes 663560 | tf_op jit(solution)/shard_map/ppermute | solution.py:460
  40.1 1.1 %collective-permute-start.8 = (bf16[2,64,864]{2,1,0:T(8,128)(2,1)S(1)}, bf16[2,64,864]{2,1,0:T(8,128)(2,1)S(1)}, u32[]{:S(2)}, u32[]{:S(2)}) collective-permute-start(bf16[2,64,864]{2,1,0:T(8,128)(2,1)S(1)} %collective-permute-done.4.rest_3_), channel_id=1, source_target_pairs={{0,4},{1,3},{4,8},{5,1},{8,12},{9,5},{12,14},{13,9},{14,10},{15,13... | collective-permute-start | bytes 663560 | tf_op jit(solution)/shard_map/ppermute | solution.py:437
  41.2 4.5 %update.3 = bf16[864,5120]{1,0:T(8,128)(2,1)} custom-call(s32[2,64,128]{2,1,0:T(8,128)S(1)} %get-tuple-element.42.keys_ref, bf16[2,864,256]{2,1,0:T(8,128)(2,1)S(1)} %get-tuple-element.44.cols_ref), custom_call_target="tpu_custom_call" | custom-call | flops 2264924160 | bytes 8847360 | tf_op jit(solution)/shard_map/update/pallas_call | solution.py:391
  45.7 0.0 collective-permute-done.9.rest_5_
  45.7 0.0 collective-permute-done.10.rest_6_
  45.7 0.0 collective-permute-done.11.rest_7_
  45.7 0.4 collective-permute-done.8.rest_4_
  46.1 3.0 %hidden.1 = bf16[128,13824]{1,0:T(8,128)(2,1)} custom-call(bf16[2,128,48]{2,1,0:T(8,128)(2,1)S(1)} %get-tuple-element.30.left_ref, bf16[2,16,13824]{2,1,0:T(8,128)(2,1)S(1)} %get-tuple-element.45.noise_ref, bf16[2,64,864]{2,1,0:T(8,128)(2,1)S(1)} %bitcast_dynamic-update-slice_fusion.rest_0_, bf16[2,64,864]{2,1,0:T(8,128)(2,1)S(1)} %collective-permute-done.2.rest_1_, ...), custom_call_target="tpu_custom_call" | custom-call | flops 100000000 | bytes 6000000 | tf_op jit(solution)/shard_map/hidden/pallas_call | solution.py:291
  (4 shorter events, 0.0 us)
Async XLA Ops:
  0.6 9.6 %copy-start = (bf16[32,5120]{1,0:T(8,128)(2,1)S(1)}, bf16[32,5120]{1,0:T(8,128)(2,1)}, u32[]{:S(2)}) copy-start(bf16[32,5120]{1,0:T(8,128)(2,1)} %x_ref.3) | copy-start | bytes 983044
  0.6 9.6 %copy-start.3 = (s32[4]{0:T(128)S(1)}, s32[4]{0:T(128)}, u32[]{:S(2)}) copy-start(s32[4]{0:T(128)} %seeds_ref.4) | copy-start | bytes 52
  9.6 3.3 %collective-permute-start.1 = (bf16[64,864]{1,0:T(8,128)(2,1)}, bf16[64,864]{1,0:T(8,128)(2,1)S(1)}, u32[]{:S(2)}, u32[]{:S(2)}) collective-permute-start(bf16[64,864]{1,0:T(8,128)(2,1)} %get-tuple-element.25.base_ref), channel_id=1, source_target_pairs={{0,1},{1,0},{2,3},{3,2},{4,5},{5,4},{6,7},{7,6},{8,9},{9,8},{10,11... | collective-permute-start | bytes 331784 | tf_op jit(solution)/shard_map/ppermute | solution.py:443
  10.1 2.7 %collective-permute-start = (s32[8,128]{1,0:T(8,128)}, s32[8,128]{1,0:T(8,128)S(1)}, u32[]{:S(2)}, u32[]{:S(2)}) collective-permute-start(s32[8,128]{1,0:T(8,128)} %get-tuple-element.26.info_ref), channel_id=1, source_target_pairs={{0,1},{1,0},{2,3},{3,2},{4,5},{5,4},{6,7},{7,6},{8,9},{9,8},{10,11... | collective-permute-start | bytes 12296 | tf_op jit(solution)/shard_map/ppermute | solution.py:437
  10.2 0.9 %copy-start.1 = (bf16[64,864]{1,0:T(8,128)(2,1)S(1)}, bf16[64,864]{1,0:T(8,128)(2,1)}, u32[]{:S(2)}) copy-start(bf16[64,864]{1,0:T(8,128)(2,1)} %get-tuple-element.25.base_ref) | copy-start | bytes 331780
  11.1 0.7 %copy-start.2 = (s32[8,128]{1,0:T(8,128)S(1)}, s32[8,128]{1,0:T(8,128)}, u32[]{:S(2)}) copy-start(s32[8,128]{1,0:T(8,128)} %get-tuple-element.26.info_ref) | copy-start | bytes 12292
  12.9 7.0 %collective-permute-start.2 = (bf16[2,64,864]{2,1,0:T(8,128)(2,1)S(1)}, bf16[2,64,864]{2,1,0:T(8,128)(2,1)S(1)}, u32[]{:S(2)}, u32[]{:S(2)}) collective-permute-start(bf16[2,64,864]{2,1,0:T(8,128)(2,1)S(1)} %bitcast_dynamic-update-slice_fusion.rest_0_), channel_id=1, source_target_pairs={{0,4},{1,3},{4,8},{5,1},{8,12},{9,5},{12,14},{13,9},{14,10},{15,13... | collective-permute-start | bytes 663560 | tf_op jit(solution)/shard_map/ppermute | solution.py:437
  19.9 7.3 %collective-permute-start.3 = (bf16[2,64,864]{2,1,0:T(8,128)(2,1)S(1)}, bf16[2,64,864]{2,1,0:T(8,128)(2,1)S(1)}, u32[]{:S(2)}, u32[]{:S(2)}) collective-permute-start(bf16[2,64,864]{2,1,0:T(8,128)(2,1)S(1)} %collective-permute-done.2.rest_1_), channel_id=1, source_target_pairs={{0,4},{1,3},{4,8},{5,1},{8,12},{9,5},{12,14},{13,9},{14,10},{15,13... | collective-permute-start | bytes 663560 | tf_op jit(solution)/shard_map/ppermute | solution.py:437
  22.0 4.0 %collective-permute-start.5 = (s32[8,128]{1,0:T(8,128)S(1)}, s32[8,128]{1,0:T(8,128)S(1)}, u32[]{:S(2)}, u32[]{:S(2)}) collective-permute-start(s32[8,128]{1,0:T(8,128)S(1)} %add.9), channel_id=1, source_target_pairs={{0,2},{1,3},{2,0},{3,1},{4,6},{5,7},{6,4},{7,5},{8,10},{9,11},{10,... | collective-permute-start | bytes 12296 | tf_op jit(solution)/shard_map/ppermute | solution.py:437
  26.0 3.6 %collective-permute-start.6 = (s32[8,128]{1,0:T(8,128)S(1)}, s32[8,128]{1,0:T(8,128)S(1)}, u32[]{:S(2)}, u32[]{:S(2)}) collective-permute-start(s32[8,128]{1,0:T(8,128)S(1)} %add.10), channel_id=1, source_target_pairs={{0,4},{1,5},{2,6},{3,7},{4,0},{5,1},{6,2},{7,3},{8,12},{9,13},{10,... | collective-permute-start | bytes 12296 | tf_op jit(solution)/shard_map/ppermute | solution.py:437
  27.2 12.3 %collective-permute-start.4 = (bf16[2,64,864]{2,1,0:T(8,128)(2,1)S(1)}, bf16[2,64,864]{2,1,0:T(8,128)(2,1)S(1)}, u32[]{:S(2)}, u32[]{:S(2)}) collective-permute-start(bf16[2,64,864]{2,1,0:T(8,128)(2,1)S(1)} %collective-permute-done.3.rest_2_), channel_id=1, source_target_pairs={{0,4},{1,3},{4,8},{5,1},{8,12},{9,5},{12,14},{13,9},{14,10},{15,13... | collective-permute-start | bytes 663560 | tf_op jit(solution)/shard_map/ppermute | solution.py:437
  29.7 4.5 %collective-permute-start.7 = (s32[8,128]{1,0:T(8,128)S(1)}, s32[8,128]{1,0:T(8,128)S(1)}, u32[]{:S(2)}, u32[]{:S(2)}) collective-permute-start(s32[8,128]{1,0:T(8,128)S(1)} %add.11.info_ref), channel_id=1, source_target_pairs={{0,8},{1,9},{2,10},{3,11},{4,12},{5,13},{6,14},{7,15},{8,0},{9,1},... | collective-permute-start | bytes 12296 | tf_op jit(solution)/shard_map/ppermute | solution.py:437
  31.8 13.8 %collective-permute-start.9 = (bf16[2,64,864]{2,1,0:T(8,128)(2,1)S(1)}, bf16[2,64,864]{2,1,0:T(8,128)(2,1)S(1)}, u32[]{:S(2)}, u32[]{:S(2)}) collective-permute-start(bf16[2,64,864]{2,1,0:T(8,128)(2,1)S(1)} %collective-permute-done.2.rest_1_), channel_id=1, source_target_pairs={{0,1},{1,0},{2,3},{3,2},{4,5},{5,4},{6,7},{7,6},{8,9},{9,8},{10,11... | collective-permute-start | bytes 663560 | tf_op jit(solution)/shard_map/ppermute | solution.py:460
  34.2 11.5 %collective-permute-start.10 = (bf16[2,64,864]{2,1,0:T(8,128)(2,1)S(1)}, bf16[2,64,864]{2,1,0:T(8,128)(2,1)S(1)}, u32[]{:S(2)}, u32[]{:S(2)}) collective-permute-start(bf16[2,64,864]{2,1,0:T(8,128)(2,1)S(1)} %collective-permute-done.3.rest_2_), channel_id=1, source_target_pairs={{0,1},{1,0},{2,3},{3,2},{4,5},{5,4},{6,7},{7,6},{8,9},{9,8},{10,11... | collective-permute-start | bytes 663560 | tf_op jit(solution)/shard_map/ppermute | solution.py:460
  39.5 6.2 %collective-permute-start.11 = (bf16[2,64,864]{2,1,0:T(8,128)(2,1)S(1)}, bf16[2,64,864]{2,1,0:T(8,128)(2,1)S(1)}, u32[]{:S(2)}, u32[]{:S(2)}) collective-permute-start(bf16[2,64,864]{2,1,0:T(8,128)(2,1)S(1)} %collective-permute-done.4.rest_3_), channel_id=1, source_target_pairs={{0,1},{1,0},{2,3},{3,2},{4,5},{5,4},{6,7},{7,6},{8,9},{9,8},{10,11... | collective-permute-start | bytes 663560 | tf_op jit(solution)/shard_map/ppermute | solution.py:460
  40.1 6.0 %collective-permute-start.8 = (bf16[2,64,864]{2,1,0:T(8,128)(2,1)S(1)}, bf16[2,64,864]{2,1,0:T(8,128)(2,1)S(1)}, u32[]{:S(2)}, u32[]{:S(2)}) collective-permute-start(bf16[2,64,864]{2,1,0:T(8,128)(2,1)S(1)} %collective-permute-done.4.rest_3_), channel_id=1, source_target_pairs={{0,4},{1,3},{4,8},{5,1},{8,12},{9,5},{12,14},{13,9},{14,10},{15,13... | collective-permute-start | bytes 663560 | tf_op jit(solution)/shard_map/ppermute | solution.py:437
